TPU v7x, 32 devices: a whole 2x2x4 slice. The times are simulated.
32 devices in a mesh: tower: 2 (over core), batch: 16 (over z, y, x).
Axes of the slice: x: 2, y: 2, z: 4, core: 2. Of those that a mesh axis runs over, the one named last changes fastest.
Arguments:
- tokens: bfloat16 [2, 32768, 768], P('tower', 'batch'), may hold values from -6 to 6
- lengths: int32 [2, 64], P('tower', 'batch'), may hold values from 64 to 512, as said below
- prefixes: int32 [2, 64], P('tower', 'batch'), may hold values from 1 to 32
- positives: int32 [64], replicated, may hold values from 0 to 63, each once
- gain_attention: float32 [768], replicated, may hold values from 0.5 to 1.5
- query_weight: bfloat16 [768, 768], replicated, may hold values from -0.02734375 to 0.02734375
- key_weight: bfloat16 [768, 768], replicated, may hold values from -0.21875 to 0.21875
- value_weight: bfloat16 [768, 768], replicated, may hold values from -0.21875 to 0.21875
- output_weight: bfloat16 [768, 768], replicated, may hold values from -1.75 to 1.75
- bucket_bias: float32 [32, 12], replicated, may hold values from -4 to 4
- gain_feedforward: float32 [768], replicated, may hold values from 0.5 to 1.5
- widen_weight: bfloat16 [768, 3072], replicated, may hold values from -0.21875 to 0.21875
- narrow_weight: bfloat16 [3072, 768], replicated, may hold values from -0.109375 to 0.109375
- gain_final: float32 [768], replicated, may hold values from 0.5 to 1.5
Outputs:
- contrast_loss: float32 [], replicated
- score_gradient: float32 [64, 64], P('batch')
- token_gradient: bfloat16 [2, 32768, 768], P('tower', 'batch')
- grad_attention: float32 [768], replicated
- grad_query: float32 [768, 768], replicated
- grad_key: float32 [768, 768], replicated
- grad_value: float32 [768, 768], replicated
- grad_output: float32 [768, 768], replicated
- grad_bucket: float32 [32, 12], replicated
- grad_feedforward: float32 [768], replicated
- grad_widen: float32 [768, 3072], replicated
- grad_narrow: float32 [3072, 768], replicated
- grad_final: float32 [768], replicated
Inputs may be any that keep to these rules, and one draw needn't show every extreme that they name: `lengths`: sequence 0 of each side uses all 512 positions. `positives`: every document is the positive of exactly one query.
All inputs are finite; a program needn't handle non-finite values.
Results may differ from a plain program's by a relative error of at most 0.025.
The roundings to bfloat16 on the way count: a program that leaves them out, or rounds other values in their place, can miss the bound.
Values sent between devices are 32-bit elements; how exact they have to be, the bound alone decides.
A program may use at most 320 MiB of HBM per device.

v0:
```python
import jax
import jax.numpy as jnp
from jax import lax
from jax.sharding import PartitionSpec as P

epsilon = 1e-06
masked_score = -1000000000.0
score_scale = 100.0
far_steps = (12, 16, 23, 32, 46, 64, 91)
highest = lax.Precision.HIGHEST


def bucket_onehot(slot_len, bucket_count):
    places = jnp.arange(slot_len, dtype=jnp.int32)
    offset = places[None, :] - places[:, None]
    spread = jnp.abs(offset)
    far_bucket = 8 + sum(((spread >= step).astype(jnp.int32) for step in far_steps))
    bucket = jnp.where(spread < 8, spread, far_bucket) + jnp.where(
        offset > 0, bucket_count // 2, 0
    ).astype(jnp.int32)
    labels = jnp.arange(bucket_count, dtype=jnp.int32)
    return (bucket[:, :, None] == labels[None, None, :]).astype(jnp.float32)


def norm_forward(values, scale_vec):
    inverse = lax.rsqrt(jnp.mean(values * values, axis=-1, keepdims=True) + epsilon)
    return (values * inverse * scale_vec, inverse)


def norm_backward(values, inverse, scale_vec, upstream):
    scaled = upstream * scale_vec
    inner_mean = jnp.mean(scaled * values, axis=-1, keepdims=True)
    grad_values = inverse * scaled - values * (inverse * inverse * inverse) * inner_mean
    grad_scale = jnp.sum(upstream * values * inverse, axis=0)
    return (grad_values, grad_scale)


def local(
    tokens,
    lengths,
    prefixes,
    positives,
    gain_attention,
    query_weight,
    key_weight,
    value_weight,
    output_weight,
    bucket_bias,
    gain_feedforward,
    widen_weight,
    narrow_weight,
    gain_final,
):
    seqs = lengths.shape[1]
    rows = tokens.shape[1]
    slot_len = rows // seqs
    width = tokens.shape[2]
    heads = bucket_bias.shape[1]
    head_dim = query_weight.shape[1] // heads
    inner = heads * head_dim
    tokens_f = tokens[0].astype(jnp.float32)
    seq_lengths = lengths[0]
    seq_prefix = prefixes[0]
    onehot = bucket_onehot(slot_len, bucket_bias.shape[0])
    bias = jnp.einsum("ijb,bh->hij", onehot, bucket_bias, precision=highest)
    normed_f, inverse_first = norm_forward(tokens_f, gain_attention)
    normed = normed_f.astype(jnp.bfloat16)

    def project(matrix):
        projected = jnp.dot(normed, matrix, preferred_element_type=jnp.float32).astype(jnp.bfloat16)
        return projected.reshape(seqs, slot_len, heads, head_dim)

    query_all = project(query_weight)
    key_all = project(key_weight)
    value_all = project(value_weight)
    places = jnp.arange(slot_len, dtype=jnp.int32)
    valid = places[None, :] < seq_lengths[:, None]

    def score_block(query_rows, key_rows, valid_keys):
        raw_scores = jnp.einsum(
            "ihd,jhd->hij", query_rows, key_rows, preferred_element_type=jnp.float32
        )
        return jnp.where(valid_keys[None, None, :], raw_scores + bias, masked_score)

    def attend_forward(parts):
        query_rows, key_rows, value_rows, valid_keys = parts
        scores = score_block(query_rows, key_rows, valid_keys)
        row_peak = jnp.max(scores, axis=-1, keepdims=True)
        raised = jnp.exp(scores - row_peak)
        totals = jnp.sum(raised, axis=-1, keepdims=True)
        soft_low = (raised / totals).astype(jnp.bfloat16)
        context = jnp.einsum(
            "hij,jhd->ihd", soft_low, value_rows, preferred_element_type=jnp.float32
        )
        return (context.astype(jnp.bfloat16), (row_peak + jnp.log(totals))[:, :, 0])

    context, log_totals = lax.map(attend_forward, (query_all, key_all, value_all, valid))
    context_flat = context.reshape(rows, inner)
    mixed = tokens_f + jnp.dot(context_flat, output_weight, preferred_element_type=jnp.float32)
    ffn_in_f, inverse_second = norm_forward(mixed, gain_feedforward)
    ffn_in = ffn_in_f.astype(jnp.bfloat16)
    pre_act = jnp.dot(ffn_in, widen_weight, preferred_element_type=jnp.float32)
    hidden = jnp.where(pre_act > 0, pre_act, 0.0).astype(jnp.bfloat16)
    output = mixed + jnp.dot(hidden, narrow_weight, preferred_element_type=jnp.float32)
    final, inverse_third = norm_forward(output, gain_final)
    pool_mask = ((places[None, :] >= seq_prefix[:, None]) & valid).astype(jnp.float32)
    pool_weight = pool_mask / jnp.sum(pool_mask, axis=1, keepdims=True)
    pooled = jnp.sum(final.reshape(seqs, slot_len, width) * pool_weight[:, :, None], axis=1)
    inverse_pool = lax.rsqrt(jnp.sum(pooled * pooled, axis=-1, keepdims=True) + epsilon)
    unit = pooled * inverse_pool
    gathered = lax.all_gather(unit, ("tower", "batch"), axis=0, tiled=True)
    total_seqs = gathered.shape[0] // 2
    query_units = gathered[:total_seqs]
    doc_units = gathered[total_seqs:]
    scores = score_scale * jnp.dot(query_units, doc_units.T, precision=highest)
    labels = jnp.arange(total_seqs, dtype=jnp.int32)
    target = (positives[:, None] == labels[None, :]).astype(jnp.float32)
    row_peak = jnp.max(scores, axis=1, keepdims=True)
    row_raised = jnp.exp(scores - row_peak)
    row_sum = jnp.sum(row_raised, axis=1, keepdims=True)
    col_peak = jnp.max(scores, axis=0, keepdims=True)
    col_raised = jnp.exp(scores - col_peak)
    col_sum = jnp.sum(col_raised, axis=0, keepdims=True)
    loss_value = (
        0.5 * jnp.sum(row_peak[:, 0] + jnp.log(row_sum[:, 0]))
        + 0.5 * jnp.sum(col_peak[0] + jnp.log(col_sum[0]))
        - jnp.sum(target * scores)
    )
    score_grad = 0.5 * row_raised / row_sum + 0.5 * col_raised / col_sum - target
    tower = lax.axis_index("tower")
    first_row = lax.axis_index("batch") * seqs
    my_rows = lax.dynamic_slice_in_dim(score_grad, first_row, seqs, 0)
    my_cols = lax.dynamic_slice_in_dim(score_grad, first_row, seqs, 1)
    grad_as_query = score_scale * jnp.dot(my_rows, doc_units, precision=highest)
    grad_as_doc = score_scale * jnp.dot(my_cols.T, query_units, precision=highest)
    grad_unit = jnp.where(tower == 0, grad_as_query, grad_as_doc)
    cubed = inverse_pool * inverse_pool * inverse_pool
    grad_pooled = inverse_pool * grad_unit - pooled * cubed * jnp.sum(
        grad_unit * pooled, axis=-1, keepdims=True
    )
    grad_fin = (pool_weight[:, :, None] * grad_pooled[:, None, :]).reshape(rows, width)
    grad_out, grad_final = norm_backward(output, inverse_third, gain_final, grad_fin)
    grad_branch = grad_out.astype(jnp.bfloat16)
    grad_narrow = jnp.einsum("tf,td->fd", hidden, grad_branch, preferred_element_type=jnp.float32)
    grad_hidden = jnp.einsum(
        "td,fd->tf", grad_branch, narrow_weight, preferred_element_type=jnp.float32
    )
    grad_pre = jnp.where(pre_act > 0, grad_hidden, 0.0).astype(jnp.bfloat16)
    grad_widen = jnp.einsum("td,tf->df", ffn_in, grad_pre, preferred_element_type=jnp.float32)
    grad_ffn_in = jnp.einsum(
        "tf,df->td", grad_pre, widen_weight, preferred_element_type=jnp.float32
    )
    grad_mixed_norm, grad_feedforward = norm_backward(
        mixed, inverse_second, gain_feedforward, grad_ffn_in
    )
    grad_mixed = grad_out + grad_mixed_norm
    grad_attn = grad_mixed.astype(jnp.bfloat16)
    grad_output = jnp.einsum(
        "ti,td->id", context_flat, grad_attn, preferred_element_type=jnp.float32
    )
    grad_context = jnp.einsum(
        "td,id->ti", grad_attn, output_weight, preferred_element_type=jnp.float32
    )
    grad_context = grad_context.astype(jnp.bfloat16).reshape(seqs, slot_len, heads, head_dim)

    def attend_backward(bias_total, parts):
        query_rows, key_rows, value_rows, valid_keys, log_rows, context_grad = parts
        scores_here = score_block(query_rows, key_rows, valid_keys)
        soft = jnp.exp(scores_here - log_rows[:, :, None])
        soft_low = soft.astype(jnp.bfloat16)
        value_part = jnp.einsum(
            "hij,ihd->jhd", soft_low, context_grad, preferred_element_type=jnp.float32
        )
        grad_soft = jnp.einsum(
            "ihd,jhd->hij", context_grad, value_rows, preferred_element_type=jnp.float32
        )
        grad_scores = soft * (grad_soft - jnp.sum(grad_soft * soft, axis=-1, keepdims=True))
        scores_low = grad_scores.astype(jnp.bfloat16)
        query_part = jnp.einsum(
            "hij,jhd->ihd", scores_low, key_rows, preferred_element_type=jnp.float32
        )
        key_part = jnp.einsum(
            "hij,ihd->jhd", scores_low, query_rows, preferred_element_type=jnp.float32
        )
        return (
            bias_total + grad_scores,
            (
                query_part.astype(jnp.bfloat16),
                key_part.astype(jnp.bfloat16),
                value_part.astype(jnp.bfloat16),
            ),
        )

    bias_total, (query_grads, key_grads, value_grads) = lax.scan(
        attend_backward,
        jnp.zeros(bias.shape, jnp.float32),
        (query_all, key_all, value_all, valid, log_totals, grad_context),
    )
    query_grads = query_grads.reshape(rows, inner)
    key_grads = key_grads.reshape(rows, inner)
    value_grads = value_grads.reshape(rows, inner)
    grad_bucket = jnp.einsum("ijb,hij->bh", onehot, bias_total, precision=highest)
    grad_query = jnp.einsum("td,ti->di", normed, query_grads, preferred_element_type=jnp.float32)
    grad_key = jnp.einsum("td,ti->di", normed, key_grads, preferred_element_type=jnp.float32)
    grad_value = jnp.einsum("td,ti->di", normed, value_grads, preferred_element_type=jnp.float32)
    grad_normed = (
        jnp.einsum("ti,di->td", query_grads, query_weight, preferred_element_type=jnp.float32)
        + jnp.einsum("ti,di->td", key_grads, key_weight, preferred_element_type=jnp.float32)
        + jnp.einsum("ti,di->td", value_grads, value_weight, preferred_element_type=jnp.float32)
    )
    grad_tokens_norm, grad_attention = norm_backward(
        tokens_f, inverse_first, gain_attention, grad_normed
    )
    token_gradient = (grad_mixed + grad_tokens_norm).astype(jnp.bfloat16)[None]
    (
        sum_attention,
        sum_query,
        sum_key,
        sum_value,
        sum_output,
        sum_bucket,
        sum_feedforward,
        sum_widen,
        sum_narrow,
        sum_final,
    ) = lax.psum(
        (
            grad_attention,
            grad_query,
            grad_key,
            grad_value,
            grad_output,
            grad_bucket,
            grad_feedforward,
            grad_widen,
            grad_narrow,
            grad_final,
        ),
        ("tower", "batch"),
    )
    return (
        loss_value,
        my_rows,
        token_gradient,
        sum_attention,
        sum_query,
        sum_key,
        sum_value,
        sum_output,
        sum_bucket,
        sum_feedforward,
        sum_widen,
        sum_narrow,
        sum_final,
    )


def solution(mesh):
    placed = (
        P("tower", "batch", None),
        P("tower", "batch"),
        P("tower", "batch"),
        P(),
        P(),
        P(),
        P(),
        P(),
        P(),
        P(),
        P(),
        P(),
        P(),
        P(),
    )
    return jax.shard_map(
        local,
        mesh=mesh,
        in_specs=placed,
        out_specs=(
            P(),
            P("batch", None),
            P("tower", "batch", None),
            P(),
            P(),
            P(),
            P(),
            P(),
            P(),
            P(),
            P(),
            P(),
            P(),
        ),
        check_vma=False,
    )
```

profile of v0, /device:TPU:0, one launch (start us, length us, event | category | flops | bytes accessed | tf_op | source)
XLA Modules:
  0.0 1078.6 jit_solution(5208512605683882147)
XLA Ops:
  74.6 13.7 %fusion.55 = f32[12,512,512]{2,0,1:T(8,128)} fusion(s32[512,512]{1,0:T(8,128)S(1)} %fusion.93, f32[32,12]{0,1:T(8,128)S(1)} %copy-done.36), kind=kOutput, calls=%fused_computation.65 | convolution fusion | flops 1216348160 | bytes 13633024 | tf_op jit(solution)/shard_map/ijb,bh->hij/dot_general | solution.py:65
  88.2 17.3 %copy.73 = f32[12,512,512]{1,2,0:T(8,128)} copy(f32[12,512,512]{2,0,1:T(8,128)} %fusion.55) | data formatting | bytes 25165824 | tf_op jit(solution)/shard_map/while | solution.py:97
  107.6 59.8 %while.29 = (s32[]{:T(128)}, bf16[4,512,12,64]{1,3,2,0:T(8,128)(2,1)}, f32[4,12,512]{2,1,0:T(8,128)}, bf16[4,512,12,64]{1,3,2,0:T(8,128)(2,1)}, pred[4,512]{1,0:...) while((s32[]{:T(128)}, ...), condition=%wide.region_4.5_spmd, body=%wide.region_1.4_spmd.sunk | while | flops 830859264 | bytes 53685868 | solution.py:97
  108.2 8.0 fusion.177
  123.0 8.0 fusion.177
  137.7 8.0 fusion.177
  152.5 8.0 fusion.177
  179.0 13.7 %fusion.113 = f32[2048,3072]{1,0:T(8,128)} fusion(bf16[768,3072]{1,0:T(8,128)(2,1)S(1)} %bitcast.270, f32[2048,768]{1,0:T(8,128)S(1)} %get-tuple-element.306, f32[768]{0:T(1024)S(1)} %copy-done.46, f32[2048]{0:T(1024)S(1)} %get-tuple-element.298), kind=kOutput, calls=%fused_computation.170 | convolution fusion | flops 9668395008 | bytes 36187136 | tf_op jit(solution)/shard_map/dot_general | solution.py:102
  192.7 19.2 %multiply_reduce_fusion.4 = (f32[2048]{0:T(1024)S(1)}, f32[2048,768]{1,0:T(8,128)}) fusion(f32[2048,768]{1,0:T(8,128)} %copy-done.16, bf16[3072,768]{1,0:T(8,128)(2,1)} %param.30, f32[2048,3072]{1,0:T(8,128)} %fusion.113), kind=kOutput, calls=%fused_computation.101 | convolution fusion | flops 9687267328 | bytes 42475520 | tf_op jit(solution)/shard_map/dot_general | solution.py:104
  215.5 72.1 %all-gather = f32[32,4,768]{2,1,0:T(4,128)S(1)} all-gather(f32[1,4,768]{2,1,0:T(4,128)S(1)} %multiply_bitcast_fusion), channel_id=1, replica_groups=mesh['tower'=2,'batch'=16] {'tower','batch'}, dimensions={0}, use_global_device_ids=true | all-gather | bytes 405504 | tf_op jit(solution)/shard_map/all_gather | solution.py:111
  300.3 18.3 %fusion.83 = f32[3072,768]{1,0:T(8,128)} fusion(bf16[2048,768]{1,0:T(8,128)(2,1)} %fusion.82, f32[2048,3072]{1,0:T(8,128)} %fusion.113), kind=kOutput, calls=%fused_computation.110 | convolution fusion | flops 9682550784 | bytes 37748736 | tf_op jit(solution)/shard_map/tf,td->fd/dot_general | solution.py:144
  318.5 20.8 %fusion.52 = bf16[2048,3072]{1,0:T(8,128)(2,1)} fusion(f32[2048,3072]{1,0:T(8,128)} %fusion.113, bf16[2048,768]{1,0:T(8,128)(2,1)} %fusion.82, bf16[3072,768]{1,0:T(8,128)(2,1)} %param.30), kind=kOutput, calls=%fused_computation.62 | convolution fusion | flops 9682550784 | bytes 45613056 | tf_op jit(solution)/shard_map/td,fd->tf/dot_general | solution.py:145
  339.4 17.4 %multiply_reduce_fusion.1 = (f32[768]{0:T(1024)}, f32[2048]{0:T(1024)S(1)}, f32[2048,768]{1,0:T(8,128)}) fusion(f32[2048,768]{1,0:T(8,128)S(1)} %bitcast.254, f32[2048]{0:T(1024)S(1)} %get-tuple-element.298, f32[768]{0:T(1024)S(1)} %copy-done.46, bf16[2048,3072]{1,0:T(8,128)(2,1)} %fusion.52, bf16[768,3072]{1,0:T(8,128)(2,1)} %param.29), kind=kOutput, calls=%fused_computation.95 | convolution fusion | flops 9673110528 | bytes 29906944 | tf_op jit(solution)/shard_map/tf,df->td/dot_general | solution.py:150
  356.8 15.6 %fusion.112 = f32[768,3072]{1,0:T(8,128)} fusion(bf16[2048,3072]{1,0:T(8,128)(2,1)} %fusion.52, f32[2048,768]{1,0:T(8,128)S(1)} %bitcast.254, f32[768]{0:T(1024)S(1)} %copy-done.46, f32[2048]{0:T(1024)S(1)} %get-tuple-element.298), kind=kOutput, calls=%fused_computation.169 | convolution fusion | flops 9668395008 | bytes 28322816 | tf_op jit(solution)/shard_map/td,tf->df/dot_general | solution.py:149
  405.7 183.0 %while.30 = (s32[]{:T(128)}, f32[12,512,512]{1,2,0:T(8,128)}, bf16[4,512,12,64]{1,3,2,0:T(8,128)(2,1)}, bf16[4,512,12,64]{1,3,2,0:T(8,128)(2,1)}, bf16[4,512,12,...) while((s32[]{:T(128)}, f32[12,512,512]{1,2,0:T(8,128)}, ...), condition=%wide.region_22.23_spmd.clone, body=%wide.region_20.22_spmd.clone.sunk | while | flops 2049042432 | bytes 177863392 | solution.py:194
  406.5 8.8 subtract_exponential_fusion.5
  425.8 13.5 %fusion.188 = (bf16[12,512,512]{1,2,0:T(8,128)(2,1)}, f32[12,512,512]{1,2,0:T(8,128)}) fusion(f32[12,512,512]{1,2,0:T(8,128)S(1)} %subtract_exponential_fusion.5, f32[12,512,512]{1,2,0:T(8,128)} %get-tuple-element.446, f32[12,512]{1,0:T(8,128)S(1)} %get-tuple-element.447, f32[12,512,512]{1,2,0:T(8,128)} %get-tuple-element.492, pred[]{:T(512)S(6)} %compare.3), kind=kLoop, calls=%fused_computation.24.clone.1 | loop fusion | flops 15728640 | bytes 56647680 | tf_op jit(solution)/shard_map/while/body/eval_jaxpr/convert_element_type | solution.py:178
  449.3 8.8 subtract_exponential_fusion.5
  468.6 17.4 %fusion.188 = (bf16[12,512,512]{1,2,0:T(8,128)(2,1)}, f32[12,512,512]{1,2,0:T(8,128)}) fusion(f32[12,512,512]{1,2,0:T(8,128)S(1)} %subtract_exponential_fusion.5, f32[12,512,512]{1,2,0:T(8,128)} %get-tuple-element.446, f32[12,512]{1,0:T(8,128)S(1)} %get-tuple-element.447, f32[12,512,512]{1,2,0:T(8,128)} %get-tuple-element.492, pred[]{:T(512)S(6)} %compare.3), kind=kLoop, calls=%fused_computation.24.clone.1 | loop fusion | flops 15728640 | bytes 56647680 | tf_op jit(solution)/shard_map/while/body/eval_jaxpr/convert_element_type | solution.py:178
  496.0 8.8 subtract_exponential_fusion.5
  515.3 17.4 %fusion.188 = (bf16[12,512,512]{1,2,0:T(8,128)(2,1)}, f32[12,512,512]{1,2,0:T(8,128)}) fusion(f32[12,512,512]{1,2,0:T(8,128)S(1)} %subtract_exponential_fusion.5, f32[12,512,512]{1,2,0:T(8,128)} %get-tuple-element.446, f32[12,512]{1,0:T(8,128)S(1)} %get-tuple-element.447, f32[12,512,512]{1,2,0:T(8,128)} %get-tuple-element.492, pred[]{:T(512)S(6)} %compare.3), kind=kLoop, calls=%fused_computation.24.clone.1 | loop fusion | flops 15728640 | bytes 56647680 | tf_op jit(solution)/shard_map/while/body/eval_jaxpr/convert_element_type | solution.py:178
  542.6 8.8 subtract_exponential_fusion.5
  561.9 17.4 %fusion.188 = (bf16[12,512,512]{1,2,0:T(8,128)(2,1)}, f32[12,512,512]{1,2,0:T(8,128)}) fusion(f32[12,512,512]{1,2,0:T(8,128)S(1)} %subtract_exponential_fusion.5, f32[12,512,512]{1,2,0:T(8,128)} %get-tuple-element.446, f32[12,512]{1,0:T(8,128)S(1)} %get-tuple-element.447, f32[12,512,512]{1,2,0:T(8,128)} %get-tuple-element.492, pred[]{:T(512)S(6)} %compare.3), kind=kLoop, calls=%fused_computation.24.clone.1 | loop fusion | flops 15728640 | bytes 56647680 | tf_op jit(solution)/shard_map/while/body/eval_jaxpr/convert_element_type | solution.py:178
  617.3 18.7 %copy.84 = f32[12,512,512]{2,0,1:T(8,128)} copy(f32[12,512,512]{1,2,0:T(8,128)} %get-tuple-element.126) | data formatting | bytes 25165824 | tf_op jit(solution)/shard_map/while | solution.py:194
  638.6 8.1 fusion.126
  646.6 7.9 fusion.127
  654.5 17.5 %fusion.92 = f32[32,12]{0,1:T(8,128)S(1)} fusion(f32[12,512,512]{2,0,1:T(8,128)S(1)} %copy-done.2, s32[512,512]{1,0:T(8,128)S(1)} %copy-done.11), kind=kOutput, calls=%fused_computation.121 | convolution fusion | flops 1216348160 | bytes 13633024 | tf_op jit(solution)/shard_map/ijb,hij->bh/dot_general | solution.py:202
  672.1 9.1 fusion.71
  681.2 39.6 %all-reduce = (f32[768]{0:T(1024)}, f32[32,12]{0,1:T(8,128)}, f32[768]{0:T(1024)}, f32[768]{0:T(1024)}) all-reduce(f32[768]{0:T(1024)S(1)} %get-tuple-element.228, f32[32,12]{0,1:T(8,128)S(1)} %fusion.92, f32[768]{0:T(1024)S(1)} %copy-done.47, f32[768]{0:T(1024)S(1)} %copy-done.33), channel_id=1, replica_groups=mesh['tower'=2,'batch'=16] {'tower','batch'}, use_global_device_ids=true, to_apply=%region_25.26 | all-reduce | flops 2688 | bytes 21504 | tf_op jit(solution)/shard_map/psum | solution.py:226
  720.8 8.3 fusion.87
  729.1 320.5 %all-reduce.4.cloned.1.call-done = (f32[768,768]{1,0:T(8,128)}, f32[768,768]{1,0:T(8,128)}, f32[768,768]{1,0:T(8,128)}, f32[768,768]{1,0:T(8,128)}, f32[768,3072]{1,0:T(8,128)}, /*index=5*/f32[3072,768]{1,0:T(8,128)}) async-done(((f32[768,768]{1,0:T(8,128)}, f32[768,768]{1,0:T(8,128)}, f32[768,768]{1,0:T(8,128)}, f32[768,768]{1,0:T(8,128)}, f32[768,3072]{1,0:T(8,128)}, /*index=5*/f32[3072,768]{1,0:T(8,128)}), ...) | async-done | bytes 28311568 | tf_op jit(solution)/shard_map/psum | solution.py:226
  1057.3 9.3 copy.133
  (252 shorter events, 279.7 us)
Async XLA Ops:
  7.2 48.2 %copy-start = (bf16[768,768]{1,0:T(8,128)(2,1)S(1)}, bf16[768,768]{1,0:T(8,128)(2,1)}, u32[]{:S(2)}) copy-start(bf16[768,768]{1,0:T(8,128)(2,1)} %param.25) | copy-start | bytes 3538948
  7.2 1042.5 %all-reduce.4.cloned.1.call-start = ((), (), s32[]{:S(2)}) async-start(), calls=%async_computation | async-start | bytes 56623104 | tf_op jit(solution)/shard_map/psum | solution.py:226
  7.7 66.9 %copy-start.10 = (s32[512,512]{1,0:T(8,128)}, s32[512,512]{1,0:T(8,128)S(1)}, u32[]{:S(2)}) copy-start(s32[512,512]{1,0:T(8,128)S(1)} %fusion.93) | copy-start | bytes 3145732
  12.5 42.9 %copy-start.27 = (f32[2048]{0:T(1024)}, f32[2048]{0:T(1024)S(1)}, u32[]{:S(2)}) copy-start(f32[2048]{0:T(1024)S(1)} %get-tuple-element.296) | copy-start | bytes 24580
  25.4 10.7 copy-start.34
  25.4 10.7 copy-start.52
  64.1 10.5 copy-start.36
  192.7 19.2 %copy-start.29 = (f32[768]{0:T(1024)S(1)}, f32[768]{0:T(1024)}, u32[]{:S(2)}) copy-start(f32[768]{0:T(1024)} %param.31) | copy-start | bytes 9220
  192.7 19.2 %copy-start.31 = (f32[4,512]{1,0:T(4,128)S(1)}, f32[4,512]{1,0:T(4,128)}, u32[]{:S(2)}) copy-start(f32[4,512]{1,0:T(4,128)} %get-tuple-element.302) | copy-start | bytes 24580
  211.9 76.4 %copy-start.48 = (s32[64]{0:T(128)S(1)}, s32[64]{0:T(128)}, u32[]{:S(2)}) copy-start(s32[64]{0:T(128)} %param.21) | copy-start | bytes 772
  211.9 78.2 %copy-start.32 = (f32[1,4,4,128]{3,2,1,0:T(4,128)S(1)}, f32[1,4,4,128]{3,2,1,0:T(4,128)}, u32[]{:S(2)}) copy-start(f32[1,4,4,128]{3,2,1,0:T(4,128)} %get-tuple-element.301) | copy-start | bytes 24580
  295.3 44.0 %slice-start.5 = ((s8[6291456]{0:T(1024)(128)(4,1)}), s8[4194304]{0:T(1024)(128)(4,1)S(1)}, s32[]{:S(2)}) async-start(s8[6291456]{0:T(1024)(128)(4,1)} %bitcast.253), calls=%async_computation.6 | async-start | bytes 8388608
  300.3 39.1 %slice-start.6 = ((s8[6291456]{0:T(1024)(128)(4,1)}), s8[2097152]{0:T(1024)(128)(4,1)S(1)}, s32[]{:S(2)}) async-start(s8[6291456]{0:T(1024)(128)(4,1)} %bitcast.253), calls=%async_computation.7 | async-start | bytes 4194304
  318.5 53.8 %slice-start = ((s8[6291456]{0:T(1024)(128)(4,1)}), s8[2097152]{0:T(1024)(128)(4,1)S(1)}, s32[]{:S(2)}) async-start(s8[6291456]{0:T(1024)(128)(4,1)} %bitcast.243), calls=%async_computation.1 | async-start | bytes 4194304
  339.4 33.0 %slice-start.1 = ((s8[6291456]{0:T(1024)(128)(4,1)}), s8[4194304]{0:T(1024)(128)(4,1)S(1)}, s32[]{:S(2)}) async-start(s8[6291456]{0:T(1024)(128)(4,1)} %bitcast.243), calls=%async_computation.2 | async-start | bytes 8388608
  356.8 15.6 %copy-start.17 = (f32[2048,768]{1,0:T(8,128)S(1)}, f32[2048,768]{1,0:T(8,128)}, u32[]{:S(2)}) copy-start(f32[2048,768]{1,0:T(8,128)} %get-tuple-element.312) | copy-start | bytes 18874372
  406.5 8.8 copy-start.3
  449.3 8.8 copy-start.3
  617.2 18.7 %copy-start.38 = (f32[64]{0:T(128)S(1)}, f32[64]{0:T(128)}, u32[]{:S(2)}) copy-start(f32[64]{0:T(128)} %copy-done.37) | copy-start | bytes 772
  617.2 18.7 %copy-start.40 = (f32[64]{0:T(128)S(1)}, f32[64]{0:T(128)}, u32[]{:S(2)}) copy-start(f32[64]{0:T(128)} %copy-done.39) | copy-start | bytes 772
  617.3 18.7 %copy-start.43 = (f32[64]{0:T(128)S(1)}, f32[64]{0:T(128)}, u32[]{:S(2)}) copy-start(f32[64]{0:T(128)} %copy-done.42) | copy-start | bytes 772
  617.3 18.7 %copy-start.45 = (f32[64]{0:T(128)S(1)}, f32[64]{0:T(128)}, u32[]{:S(2)}) copy-start(f32[64]{0:T(128)} %copy-done.44) | copy-start | bytes 772
  617.3 21.3 %copy-start.51 = (bf16[768,768]{1,0:T(8,128)(2,1)S(1)}, bf16[768,768]{1,0:T(8,128)(2,1)}, u32[]{:S(2)}) copy-start(bf16[768,768]{1,0:T(8,128)(2,1)} %param.23) | copy-start | bytes 3538948
  638.5 16.0 %copy-start.2 = (f32[12,512,512]{2,0,1:T(8,128)S(1)}, f32[12,512,512]{2,0,1:T(8,128)}, u32[]{:S(2)}) copy-start(f32[12,512,512]{2,0,1:T(8,128)} %copy.84) | copy-start | bytes 37748740
  654.5 17.5 %copy-start.8 = (bf16[1,2048,768]{2,1,0:T(8,128)(2,1)S(1)}, bf16[1,2048,768]{2,1,0:T(8,128)(2,1)}, u32[]{:S(2)}) copy-start(bf16[1,2048,768]{2,1,0:T(8,128)(2,1)} %param.18) | copy-start | bytes 9437188
  654.5 17.5 %copy-start.15 = (bf16[96,8,4,512]{3,1,2,0:T(8,128)(2,1)S(1)}, bf16[96,8,4,512]{3,1,2,0:T(8,128)(2,1)}, u32[]{:S(2)}) copy-start(bf16[96,8,4,512]{3,1,2,0:T(8,128)(2,1)} %copy-done.14) | copy-start | bytes 9437188
  672.1 9.1 copy-start.33
  672.1 9.1 copy-start.47
  672.1 48.7 %copy-start.30 = (f32[2048]{0:T(1024)S(1)}, f32[2048]{0:T(1024)}, u32[]{:S(2)}) copy-start(f32[2048]{0:T(1024)} %get-tuple-element.295) | copy-start | bytes 24580
  1055.9 10.7 slice-start.2
  1057.3 9.3 slice-start.3
  1057.3 9.3 slice-start.4
  (37 other events, 191.2 us)
Sparse Core Ops, SparseCore 0:
  617.4 432.2 all-reduce.3
where the time goes:
time: 1080 us
  matrix products  366 us (34%)
  waiting for transfers between devices  321 us (30%)
  local copies, waits for them, and re-layouts  153 us (14%)
  blocking collectives  112 us (10%)
  other arithmetic  109 us (10%)
  between operations  18 us (2%)
    psum x1, waiting for transfers between devices, local(): lax.psum((grad_attention, grad_query, grad_key, grad_value, grad_output,...  321 us
    all_gather x1, blocking collectives, local(): gathered = lax.all_gather(unit, ('tower', 'batch'), axis=0, tiled=True)  72.1 us
    dot_general x8, matrix products, score_block(): jnp.einsum('ihd,jhd->hij', query_rows, key_rows, preferred_element_type=j...  67.1 us
    convert_element_type x4, other arithmetic, attend_backward(): scores_low = grad_scores.astype(jnp.bfloat16)  65.7 us
    psum x1, blocking collectives, local(): lax.psum((grad_attention, grad_query, grad_key, grad_value, grad_output,...  39.6 us
    while x5, local copies, waits for them, and re-layouts, local(): lax.map(attend_forward, (query_all, key_all, value_all, valid))  35 us
    unnamed x132, local copies, waits for them, and re-layouts  34.2 us
    dot_general x4, matrix products, attend_backward(): jnp.einsum('ihd,jhd->hij', context_grad, value_rows, preferred_element_ty...  30 us
  transfers between devices with their start and end apart: 1, of which 1 were waited for; matrix products, arithmetic and copies ran while one was open for 7% of the time, Pallas kernels for 0%

commit v1 on v0

--- a/solution.py
+++ b/solution.py
@@ -224,19 +224,22 @@
         sum_narrow,
         sum_final,
     ) = lax.psum(
-        (
-            grad_attention,
-            grad_query,
-            grad_key,
-            grad_value,
-            grad_output,
-            grad_bucket,
-            grad_feedforward,
-            grad_widen,
-            grad_narrow,
-            grad_final,
+        lax.psum(
+            (
+                grad_attention,
+                grad_query,
+                grad_key,
+                grad_value,
+                grad_output,
+                grad_bucket,
+                grad_feedforward,
+                grad_widen,
+                grad_narrow,
+                grad_final,
+            ),
+            "batch",
         ),
-        ("tower", "batch"),
+        "tower",
     )
     return (
         loss_value,

time: 1080 us -> 1560 us (1.44)
  waiting for transfers between devices: 321 us -> 748 us
  blocking collectives: 112 us -> 151 us
    psum x1, waiting for transfers between devices: 321 us -> 748 us  [local(): lax.psum((grad_attention, grad_query, grad_key, grad_value, grad_output,...]
    psum x1, blocking collectives: 39.6 us -> 75 us  [local(): lax.psum((grad_attention, grad_query, grad_key, grad_value, grad_output,...]
  transfers between devices with their start and end apart: 1 -> 2, of which waited for: 1 -> 1; matrix products, arithmetic and copies ran while one was open for 7% -> 5% of each run, Pallas kernels for 0% -> 0%
where the time goes in v1:
time: 1560 us; the launch traced here: 1550 us
  waiting for transfers between devices  748 us (48%)
  matrix products  370 us (24%)
  local copies, waits for them, and re-layouts  154 us (10%)
  blocking collectives  151 us (10%)
  other arithmetic  109 us (7%)
  between operations  18 us (1%)
    psum x1, waiting for transfers between devices, local(): lax.psum((grad_attention, grad_query, grad_key, grad_value, grad_output,...  748 us
    psum x1, blocking collectives, local(): lax.psum((grad_attention, grad_query, grad_key, grad_value, grad_output,...  75 us
    all_gather x1, blocking collectives, local(): gathered = lax.all_gather(unit, ('tower', 'batch'), axis=0, tiled=True)  72.1 us
    dot_general x8, matrix products, score_block(): jnp.einsum('ihd,jhd->hij', query_rows, key_rows, preferred_element_type=j...  67.1 us
    convert_element_type x4, other arithmetic, attend_backward(): scores_low = grad_scores.astype(jnp.bfloat16)  66.2 us
    while x5, local copies, waits for them, and re-layouts, local(): lax.map(attend_forward, (query_all, key_all, value_all, valid))  35.3 us
    unnamed x132, local copies, waits for them, and re-layouts  34.2 us
  transfers between devices with their start and end apart: 2, of which 1 were waited for; matrix products, arithmetic and copies ran while one was open for 5% of the time, Pallas kernels for 0%

profile of v1, /device:TPU:0, one launch (start us, length us, event | category | flops | bytes accessed | tf_op | source)
XLA Modules:
  0.0 1551.7 jit_solution(15842778743503892094)
XLA Ops:
  74.6 13.7 fusion.55
  88.2 17.6 %copy.73 = f32[12,512,512]{1,2,0:T(8,128)} copy(f32[12,512,512]{2,0,1:T(8,128)} %fusion.55) | data formatting | bytes 25165824 | tf_op jit(solution)/shard_map/while | solution.py:97
  107.9 59.8 %while.29 = (s32[]{:T(128)}, bf16[4,512,12,64]{1,3,2,0:T(8,128)(2,1)}, f32[4,12,512]{2,1,0:T(8,128)}, bf16[4,512,12,64]{1,3,2,0:T(8,128)(2,1)}, pred[4,512]{1,0:...) while((s32[]{:T(128)}, ...), condition=%wide.region_4.5_spmd, body=%wide.region_1.4_spmd.sunk | while | flops 830859264 | bytes 53685868 | solution.py:97
  108.5 8.0 fusion.177
  123.2 8.0 fusion.177
  138.0 8.0 fusion.177
  152.8 8.0 fusion.177
  179.3 13.8 fusion.113
  193.1 19.2 %multiply_reduce_fusion.4 = (f32[2048]{0:T(1024)S(1)}, f32[2048,768]{1,0:T(8,128)}) fusion(f32[2048,768]{1,0:T(8,128)} %copy-done.16, bf16[3072,768]{1,0:T(8,128)(2,1)} %param.30, f32[2048,3072]{1,0:T(8,128)} %fusion.113), kind=kOutput, calls=%fused_computation.101 | convolution fusion | flops 9687267328 | bytes 42475520 | tf_op jit(solution)/shard_map/dot_general | solution.py:104
  215.9 72.1 %all-gather = f32[32,4,768]{2,1,0:T(4,128)S(1)} all-gather(f32[1,4,768]{2,1,0:T(4,128)S(1)} %multiply_bitcast_fusion), channel_id=1, replica_groups=mesh['tower'=2,'batch'=16] {'tower','batch'}, dimensions={0}, use_global_device_ids=true | all-gather | bytes 405504 | tf_op jit(solution)/shard_map/all_gather | solution.py:111
  300.6 18.3 %fusion.83 = f32[3072,768]{1,0:T(8,128)} fusion(bf16[2048,768]{1,0:T(8,128)(2,1)} %fusion.82, f32[2048,3072]{1,0:T(8,128)} %fusion.113), kind=kOutput, calls=%fused_computation.110 | convolution fusion | flops 9682550784 | bytes 37748736 | tf_op jit(solution)/shard_map/tf,td->fd/dot_general | solution.py:144
  318.9 21.0 %fusion.52 = bf16[2048,3072]{1,0:T(8,128)(2,1)} fusion(f32[2048,3072]{1,0:T(8,128)} %fusion.113, bf16[2048,768]{1,0:T(8,128)(2,1)} %fusion.82, bf16[3072,768]{1,0:T(8,128)(2,1)} %param.30), kind=kOutput, calls=%fused_computation.62 | convolution fusion | flops 9682550784 | bytes 45613056 | tf_op jit(solution)/shard_map/td,fd->tf/dot_general | solution.py:145
  339.9 17.4 %multiply_reduce_fusion.1 = (f32[768]{0:T(1024)}, f32[2048]{0:T(1024)S(1)}, f32[2048,768]{1,0:T(8,128)}) fusion(f32[2048,768]{1,0:T(8,128)S(1)} %bitcast.254, f32[2048]{0:T(1024)S(1)} %get-tuple-element.308, f32[768]{0:T(1024)S(1)} %copy-done.46, bf16[2048,3072]{1,0:T(8,128)(2,1)} %fusion.52, bf16[768,3072]{1,0:T(8,128)(2,1)} %param.29), kind=kOutput, calls=%fused_computation.95 | convolution fusion | flops 9673110528 | bytes 29906944 | tf_op jit(solution)/shard_map/tf,df->td/dot_general | solution.py:150
  357.3 15.6 %fusion.112 = f32[768,3072]{1,0:T(8,128)} fusion(bf16[2048,3072]{1,0:T(8,128)(2,1)} %fusion.52, f32[2048,768]{1,0:T(8,128)S(1)} %bitcast.254, f32[768]{0:T(1024)S(1)} %copy-done.46, f32[2048]{0:T(1024)S(1)} %get-tuple-element.308), kind=kOutput, calls=%fused_computation.169 | convolution fusion | flops 9668395008 | bytes 28322816 | tf_op jit(solution)/shard_map/td,tf->df/dot_general | solution.py:149
  406.3 183.2 %while.30 = (s32[]{:T(128)}, f32[12,512,512]{1,2,0:T(8,128)}, bf16[4,512,12,64]{1,3,2,0:T(8,128)(2,1)}, bf16[4,512,12,64]{1,3,2,0:T(8,128)(2,1)}, bf16[4,512,12,...) while((s32[]{:T(128)}, f32[12,512,512]{1,2,0:T(8,128)}, ...), condition=%wide.region_22.23_spmd.clone, body=%wide.region_20.22_spmd.clone.sunk | while | flops 2049042432 | bytes 177863392 | solution.py:194
  407.1 8.8 subtract_exponential_fusion.5
  426.3 13.6 fusion.188
  449.9 8.8 subtract_exponential_fusion.5
  469.1 17.5 %fusion.188 = (bf16[12,512,512]{1,2,0:T(8,128)(2,1)}, f32[12,512,512]{1,2,0:T(8,128)}) fusion(f32[12,512,512]{1,2,0:T(8,128)S(1)} %subtract_exponential_fusion.5, f32[12,512,512]{1,2,0:T(8,128)} %get-tuple-element.456, f32[12,512]{1,0:T(8,128)S(1)} %get-tuple-element.457, f32[12,512,512]{1,2,0:T(8,128)} %get-tuple-element.502, pred[]{:T(512)S(6)} %compare.3), kind=kLoop, calls=%fused_computation.24.clone.1 | loop fusion | flops 15728640 | bytes 56647680 | tf_op jit(solution)/shard_map/while/body/eval_jaxpr/convert_element_type | solution.py:178
  496.7 8.8 subtract_exponential_fusion.5
  515.9 17.5 %fusion.188 = (bf16[12,512,512]{1,2,0:T(8,128)(2,1)}, f32[12,512,512]{1,2,0:T(8,128)}) fusion(f32[12,512,512]{1,2,0:T(8,128)S(1)} %subtract_exponential_fusion.5, f32[12,512,512]{1,2,0:T(8,128)} %get-tuple-element.456, f32[12,512]{1,0:T(8,128)S(1)} %get-tuple-element.457, f32[12,512,512]{1,2,0:T(8,128)} %get-tuple-element.502, pred[]{:T(512)S(6)} %compare.3), kind=kLoop, calls=%fused_computation.24.clone.1 | loop fusion | flops 15728640 | bytes 56647680 | tf_op jit(solution)/shard_map/while/body/eval_jaxpr/convert_element_type | solution.py:178
  543.4 8.8 subtract_exponential_fusion.5
  562.7 17.5 %fusion.188 = (bf16[12,512,512]{1,2,0:T(8,128)(2,1)}, f32[12,512,512]{1,2,0:T(8,128)}) fusion(f32[12,512,512]{1,2,0:T(8,128)S(1)} %subtract_exponential_fusion.5, f32[12,512,512]{1,2,0:T(8,128)} %get-tuple-element.456, f32[12,512]{1,0:T(8,128)S(1)} %get-tuple-element.457, f32[12,512,512]{1,2,0:T(8,128)} %get-tuple-element.502, pred[]{:T(512)S(6)} %compare.3), kind=kLoop, calls=%fused_computation.24.clone.1 | loop fusion | flops 15728640 | bytes 56647680 | tf_op jit(solution)/shard_map/while/body/eval_jaxpr/convert_element_type | solution.py:178
  618.2 748.5 %all-reduce.7.cloned.1.call-done = (f32[768,768]{1,0:T(8,128)}, f32[768,768]{1,0:T(8,128)}, f32[768,768]{1,0:T(8,128)}, f32[768,768]{1,0:T(8,128)}, f32[768,3072]{1,0:T(8,128)}, /*index=5*/f32[3072,768]{1,0:T(8,128)}) async-done(((f32[768,768]{1,0:T(8,128)}, f32[768,768]{1,0:T(8,128)}, f32[768,768]{1,0:T(8,128)}, f32[768,768]{1,0:T(8,128)}, f32[768,3072]{1,0:T(8,128)}, /*index=5*/f32[3072,768]{1,0:T(8,128)}), ...) | async-done | bytes 28311568 | tf_op jit(solution)/shard_map/psum | solution.py:227
  1366.7 19.2 %copy.84 = f32[12,512,512]{2,0,1:T(8,128)} copy(f32[12,512,512]{1,2,0:T(8,128)} %get-tuple-element.126) | data formatting | bytes 25165824 | tf_op jit(solution)/shard_map/while | solution.py:194
  1388.5 9.1 fusion.126
  1397.7 10.3 fusion.127
  1408.0 17.5 %fusion.92 = f32[32,12]{0,1:T(8,128)S(1)} fusion(f32[12,512,512]{2,0,1:T(8,128)S(1)} %copy-done.2, s32[512,512]{1,0:T(8,128)S(1)} %copy-done.11), kind=kOutput, calls=%fused_computation.121 | convolution fusion | flops 1216348160 | bytes 13633024 | tf_op jit(solution)/shard_map/ijb,hij->bh/dot_general | solution.py:202
  1425.5 10.2 fusion.71
  1435.7 75.0 %all-reduce = (f32[768]{0:T(1024)S(1)}, f32[32,12]{0,1:T(8,128)S(1)}, f32[768]{0:T(1024)S(1)}, f32[768]{0:T(1024)S(1)}) all-reduce(f32[768]{0:T(1024)S(1)} %get-tuple-element.228, f32[32,12]{0,1:T(8,128)S(1)} %fusion.92, f32[768]{0:T(1024)S(1)} %copy-done.47, f32[768]{0:T(1024)S(1)} %copy-done.33), channel_id=1, replica_groups=mesh['tower'=2,'batch'=16] {'batch'}, use_global_device_ids=true, to_apply=%region_25.26 | all-reduce | flops 2688 | bytes 21504 | tf_op jit(solution)/shard_map/psum | solution.py:227
  1514.7 8.1 fusion.87
  1530.5 9.3 copy.139
  (256 shorter events, 283.6 us)
Async XLA Ops:
  7.2 48.2 %copy-start = (bf16[768,768]{1,0:T(8,128)(2,1)S(1)}, bf16[768,768]{1,0:T(8,128)(2,1)}, u32[]{:S(2)}) copy-start(bf16[768,768]{1,0:T(8,128)(2,1)} %param.25) | copy-start | bytes 3538948
  7.2 1359.4 %all-reduce.7.cloned.1.call-start = ((), (), s32[]{:S(2)}) async-start(), calls=%async_computation | async-start | bytes 56623104 | tf_op jit(solution)/shard_map/psum | solution.py:227
  7.7 66.9 %copy-start.10 = (s32[512,512]{1,0:T(8,128)}, s32[512,512]{1,0:T(8,128)S(1)}, u32[]{:S(2)}) copy-start(s32[512,512]{1,0:T(8,128)S(1)} %fusion.93) | copy-start | bytes 3145732
  12.5 42.9 %copy-start.27 = (f32[2048]{0:T(1024)}, f32[2048]{0:T(1024)S(1)}, u32[]{:S(2)}) copy-start(f32[2048]{0:T(1024)S(1)} %get-tuple-element.306) | copy-start | bytes 24580
  25.4 10.7 copy-start.34
  25.4 10.7 copy-start.52
  64.1 10.5 copy-start.36
  193.1 19.2 %copy-start.29 = (f32[768]{0:T(1024)S(1)}, f32[768]{0:T(1024)}, u32[]{:S(2)}) copy-start(f32[768]{0:T(1024)} %param.31) | copy-start | bytes 9220
  193.1 19.2 %copy-start.31 = (f32[4,512]{1,0:T(4,128)S(1)}, f32[4,512]{1,0:T(4,128)}, u32[]{:S(2)}) copy-start(f32[4,512]{1,0:T(4,128)} %get-tuple-element.312) | copy-start | bytes 24580
  212.3 76.4 %copy-start.48 = (s32[64]{0:T(128)S(1)}, s32[64]{0:T(128)}, u32[]{:S(2)}) copy-start(s32[64]{0:T(128)} %param.21) | copy-start | bytes 772
  212.3 78.2 %copy-start.32 = (f32[1,4,4,128]{3,2,1,0:T(4,128)S(1)}, f32[1,4,4,128]{3,2,1,0:T(4,128)}, u32[]{:S(2)}) copy-start(f32[1,4,4,128]{3,2,1,0:T(4,128)} %get-tuple-element.311) | copy-start | bytes 24580
  295.7 44.2 %slice-start.5 = ((s8[6291456]{0:T(1024)(128)(4,1)}), s8[4194304]{0:T(1024)(128)(4,1)S(1)}, s32[]{:S(2)}) async-start(s8[6291456]{0:T(1024)(128)(4,1)} %bitcast.253), calls=%async_computation.7 | async-start | bytes 8388608
  300.6 39.2 %slice-start.6 = ((s8[6291456]{0:T(1024)(128)(4,1)}), s8[2097152]{0:T(1024)(128)(4,1)S(1)}, s32[]{:S(2)}) async-start(s8[6291456]{0:T(1024)(128)(4,1)} %bitcast.253), calls=%async_computation.8 | async-start | bytes 4194304
  318.9 54.0 %slice-start = ((s8[6291456]{0:T(1024)(128)(4,1)}), s8[2097152]{0:T(1024)(128)(4,1)S(1)}, s32[]{:S(2)}) async-start(s8[6291456]{0:T(1024)(128)(4,1)} %bitcast.243), calls=%async_computation.2 | async-start | bytes 4194304
  339.9 33.0 %slice-start.1 = ((s8[6291456]{0:T(1024)(128)(4,1)}), s8[4194304]{0:T(1024)(128)(4,1)S(1)}, s32[]{:S(2)}) async-start(s8[6291456]{0:T(1024)(128)(4,1)} %bitcast.243), calls=%async_computation.3 | async-start | bytes 8388608
  357.3 15.6 %copy-start.17 = (f32[2048,768]{1,0:T(8,128)S(1)}, f32[2048,768]{1,0:T(8,128)}, u32[]{:S(2)}) copy-start(f32[2048,768]{1,0:T(8,128)} %get-tuple-element.322) | copy-start | bytes 18874372
  618.1 904.7 %all-reduce.9.cloned.1.call-start = ((), (), s32[]{:S(2)}) async-start(), calls=%async_computation.1 | async-start | bytes 56623104 | tf_op jit(solution)/shard_map/psum | solution.py:226
  1366.6 19.3 %copy-start.38 = (f32[64]{0:T(128)S(1)}, f32[64]{0:T(128)}, u32[]{:S(2)}) copy-start(f32[64]{0:T(128)} %copy-done.37) | copy-start | bytes 772
  1366.7 19.3 %copy-start.40 = (f32[64]{0:T(128)S(1)}, f32[64]{0:T(128)}, u32[]{:S(2)}) copy-start(f32[64]{0:T(128)} %copy-done.39) | copy-start | bytes 772
  1366.7 19.3 %copy-start.43 = (f32[64]{0:T(128)S(1)}, f32[64]{0:T(128)}, u32[]{:S(2)}) copy-start(f32[64]{0:T(128)} %copy-done.42) | copy-start | bytes 772
  1366.7 19.3 %copy-start.45 = (f32[64]{0:T(128)S(1)}, f32[64]{0:T(128)}, u32[]{:S(2)}) copy-start(f32[64]{0:T(128)} %copy-done.44) | copy-start | bytes 772
  1366.7 21.8 %copy-start.51 = (bf16[768,768]{1,0:T(8,128)(2,1)S(1)}, bf16[768,768]{1,0:T(8,128)(2,1)}, u32[]{:S(2)}) copy-start(bf16[768,768]{1,0:T(8,128)(2,1)} %param.23) | copy-start | bytes 3538948
  1388.5 19.4 %copy-start.2 = (f32[12,512,512]{2,0,1:T(8,128)S(1)}, f32[12,512,512]{2,0,1:T(8,128)}, u32[]{:S(2)}) copy-start(f32[12,512,512]{2,0,1:T(8,128)} %copy.84) | copy-start | bytes 37748740
  1397.7 10.3 copy-start.11
  1407.9 17.5 %copy-start.8 = (bf16[1,2048,768]{2,1,0:T(8,128)(2,1)S(1)}, bf16[1,2048,768]{2,1,0:T(8,128)(2,1)}, u32[]{:S(2)}) copy-start(bf16[1,2048,768]{2,1,0:T(8,128)(2,1)} %param.18) | copy-start | bytes 9437188
  1407.9 17.5 %copy-start.15 = (bf16[96,8,4,512]{3,1,2,0:T(8,128)(2,1)S(1)}, bf16[96,8,4,512]{3,1,2,0:T(8,128)(2,1)}, u32[]{:S(2)}) copy-start(bf16[96,8,4,512]{3,1,2,0:T(8,128)(2,1)} %copy-done.14) | copy-start | bytes 9437188
  1425.5 10.2 copy-start.33
  1425.5 10.2 copy-start.47
  1425.5 89.2 %copy-start.30 = (f32[2048]{0:T(1024)S(1)}, f32[2048]{0:T(1024)}, u32[]{:S(2)}) copy-start(f32[2048]{0:T(1024)} %get-tuple-element.305) | copy-start | bytes 24580
  1529.1 10.7 slice-start.2
  1530.5 9.3 slice-start.3
  1530.5 9.3 slice-start.4
  (38 other events, 200.9 us)
Sparse Core Ops, SparseCore 0:
  618.2 748.3 all-reduce.6
  1370.1 90.4 all-reduce.8
